TPU v7x, 32 devices: a whole 2x2x4 slice. The times are simulated.
32 devices in a mesh: seq: 8 (over z, x), tp: 4 (over y, core).
Axes of the slice: x: 2, y: 2, z: 4, core: 2. Of those that a mesh axis runs over, the one named last changes fastest.
Arguments:
- hidden_new: bfloat16 [3, 16, 8192], P(None, None, 'seq'), may hold values from -6 to 6
- w_kv: bfloat16 [8192, 8, 256], P('seq', 'tp'), may hold values from -0.0625 to 0.0625
- w_out: bfloat16 [8192, 8192], P('tp', 'seq'), may hold values from -0.0625 to 0.0625
- queries_draft: bfloat16 [3, 4, 8, 32, 128], P(None, None, 'tp'), may hold values from -48 to 48
- queries_verify: bfloat16 [3, 4, 8, 32, 128], P(None, None, 'tp'), may hold values from -48 to 48
- keys_cache: bfloat16 [4, 8, 16384, 128], P(None, 'tp', 'seq'), may hold values from -6 to 6
- values_cache: bfloat16 [4, 8, 16384, 128], P(None, 'tp', 'seq'), may hold values from -6 to 6
- key_levels: bfloat16 [4, 8, 16384, 128], P(None, 'tp', 'seq'), may hold values from -8 to 7, as said below
- value_levels: bfloat16 [4, 8, 16384, 128], P(None, 'tp', 'seq'), may hold values from -8 to 7, as said below
- key_scales: float32 [4, 8, 16384], P(None, 'tp', 'seq'), may hold values from 0.05 to 0.5
- value_scales: float32 [4, 8, 16384], P(None, 'tp', 'seq'), may hold values from 0.1 to 0.4
- lengths: int32 [4], replicated, may hold values from 2 to 16376, as said below
- accepted: int32 [2, 4], replicated, may hold values from 0 to 4, as said below
Outputs:
- layer_out: bfloat16 [3, 2, 16, 8192], P(None, None, None, 'seq')
Inputs may be any that keep to these rules, and one draw needn't show every extreme that they name: `key_levels`: every entry is a whole number. Positions 0 and 1 of every sequence and head hold equal levels. `value_levels`: every entry is a whole number. `lengths`: some sequence starts with exactly 16376 valid positions, another with 16 or fewer. `accepted`: the values 0 and 4 both occur.
All inputs are finite; a program needn't handle non-finite values.
Results may differ from a plain program's by a relative error of at most 0.006.
The roundings to bfloat16 on the way count: a program that leaves them out, or rounds other values in their place, can miss the bound.
Values may be sent and summed in bfloat16 or wider, within the bound.
A program may use at most 128 MiB of HBM per device.

v0:
```python
import math
import jax
import jax.numpy as jnp
from jax import lax
from jax.sharding import PartitionSpec as P

HD = 128
GROUP = 8
R = 4
ROUNDS = 3
NEG = -1e30


def dequantize(levels, scales):
    return (levels.astype(jnp.float32) * scales[..., None]).astype(jnp.bfloat16)


def attend(queries, keys, values, usable):
    scores = jnp.einsum("bhqd,bhkd->bhqk", queries, keys, preferred_element_type=jnp.float32) * (
        1.0 / math.sqrt(HD)
    )
    scores = jnp.where(usable, scores, NEG)
    maxima = jnp.max(scores, axis=-1)
    weights = jnp.where(usable, jnp.exp(scores - maxima[..., None]), 0.0).astype(jnp.bfloat16)
    totals = jnp.sum(weights.astype(jnp.float32), axis=-1)
    weighted = jnp.einsum("bhqk,bhkd->bhqd", weights, values, preferred_element_type=jnp.float32)
    return (maxima, totals, weighted)


def combine(former, latter):
    highest = jnp.maximum(former[0], latter[0])
    former_w = jnp.exp(former[0] - highest)
    latter_w = jnp.exp(latter[0] - highest)
    return (
        highest,
        former[1] * former_w + latter[1] * latter_w,
        former[2] * former_w[..., None] + latter[2] * latter_w[..., None],
    )


def finish(partial_value):
    return (partial_value[2] / partial_value[1][..., None]).astype(jnp.bfloat16)


def arrange(attended):
    kind_count, batch_size, head_count, query_rows, head_width = attended.shape
    split_rows = attended.reshape(kind_count, batch_size, head_count, GROUP, R, head_width)
    return split_rows.transpose(0, 1, 4, 2, 3, 5).reshape(
        kind_count * batch_size * R, head_count * GROUP * head_width
    )


def stacked_rows(draft_part, verify_part):
    maxima = jnp.stack([draft_part[0], verify_part[0]]).reshape(1, -1)
    totals = jnp.stack([draft_part[1], verify_part[1]]).reshape(1, -1)
    weighted = jnp.stack([draft_part[2], verify_part[2]]).reshape(1, maxima.shape[1], -1)
    return (maxima, totals, weighted)


def spread_merge(draft_part, verify_part, draft_self, verify_self, seq_index):
    maxima, totals, weighted = stacked_rows(draft_part, verify_part)
    maxima, totals, weighted = (
        lax.all_to_all(maxima, "seq", split_axis=1, concat_axis=0, tiled=True),
        lax.all_to_all(totals, "seq", split_axis=1, concat_axis=0, tiled=True),
        lax.all_to_all(weighted, "seq", split_axis=1, concat_axis=0, tiled=True),
    )
    highest = jnp.max(maxima, axis=0)
    factors = jnp.exp(maxima - highest[None])
    share_part = (
        highest,
        jnp.sum(totals * factors, axis=0),
        jnp.sum(weighted * factors[..., None], axis=0),
    )
    share_rows = highest.shape[0]
    self_max, self_tot, self_sum = stacked_rows(draft_self, verify_self)
    row_start = seq_index * share_rows
    self_share = (
        lax.dynamic_slice_in_dim(self_max[0], row_start, share_rows, 0),
        lax.dynamic_slice_in_dim(self_tot[0], row_start, share_rows, 0),
        lax.dynamic_slice_in_dim(self_sum[0], row_start, share_rows, 0),
    )
    merged = finish(combine(share_part, self_share))
    gathered = lax.all_gather(merged, "seq", axis=0, tiled=True)
    return gathered.reshape((2,) + draft_part[2].shape)


def per_device(
    hidden_new,
    w_kv,
    w_out,
    queries_draft,
    queries_verify,
    keys_cache,
    values_cache,
    key_levels,
    value_levels,
    key_scales,
    value_scales,
    lengths,
    accepted,
):
    batch_size, head_count, local_len, head_width = keys_cache.shape
    seq_index = lax.axis_index("seq")
    first_row = seq_index * local_len
    key_low = dequantize(key_levels, key_scales)
    value_low = dequantize(value_levels, value_scales)
    places = first_row + jnp.arange(local_len, dtype=jnp.int32)
    stored = (places[None, :] < lengths[:, None])[:, None, :, None]
    flat_kv = w_kv.reshape(w_kv.shape[0], -1)
    tokens = jnp.arange(GROUP * R, dtype=jnp.int32) % R
    causal = (tokens[:, None] >= jnp.arange(R, dtype=jnp.int32)[None, :])[None, None]
    offsets = jnp.arange(R, dtype=jnp.int32)[None, :]
    batch_rows = jnp.broadcast_to(jnp.arange(batch_size, dtype=jnp.int32)[:, None], (batch_size, R))
    length_now = lengths
    results = []
    for turn_index in range(ROUNDS):
        partial_kv = jnp.dot(hidden_new[turn_index], flat_kv, preferred_element_type=jnp.float32)
        fresh_rows = (
            lax.psum(partial_kv, "seq")
            .astype(jnp.bfloat16)
            .reshape(batch_size, R, head_count, 2, head_width)
        )
        new_keys = fresh_rows[:, :, :, 0].transpose(0, 2, 1, 3)
        new_values = fresh_rows[:, :, :, 1].transpose(0, 2, 1, 3)
        usable = (places[None, :] < length_now[:, None])[:, None, None, :]
        draft_q = queries_draft[turn_index]
        verify_q = queries_verify[turn_index]
        draft_keys = jnp.where(stored, key_low, keys_cache)
        draft_values = jnp.where(stored, value_low, values_cache)
        draft_part = attend(draft_q, draft_keys, draft_values, usable)
        draft_self = attend(draft_q, new_keys, new_values, causal)
        verify_part = attend(verify_q, keys_cache, values_cache, usable)
        verify_self = attend(verify_q, new_keys, new_values, causal)
        attended = spread_merge(draft_part, verify_part, draft_self, verify_self, seq_index)
        projected = jnp.dot(arrange(attended), w_out, preferred_element_type=jnp.float32)
        summed = lax.psum(projected, "tp")
        results.append(summed.astype(jnp.bfloat16).reshape(2, batch_size * R, -1))
        if turn_index + 1 < ROUNDS:
            accepted_now = accepted[turn_index]
            targets = length_now[:, None] + offsets - first_row
            landing = (offsets < accepted_now[:, None]) & (targets >= 0) & (targets < local_len)
            targets = jnp.where(landing, targets, local_len)
            keys_cache = keys_cache.at[batch_rows, :, targets, :].set(
                fresh_rows[:, :, :, 0], mode="drop"
            )
            values_cache = values_cache.at[batch_rows, :, targets, :].set(
                fresh_rows[:, :, :, 1], mode="drop"
            )
            length_now = length_now + accepted_now
    return jnp.stack(results)


def solution(mesh):
    return jax.shard_map(
        per_device,
        mesh=mesh,
        in_specs=(
            P(None, None, "seq"),
            P("seq", "tp", None),
            P("tp", "seq"),
            P(None, None, "tp", None, None),
            P(None, None, "tp", None, None),
            P(None, "tp", "seq", None),
            P(None, "tp", "seq", None),
            P(None, "tp", "seq", None),
            P(None, "tp", "seq", None),
            P(None, "tp", "seq"),
            P(None, "tp", "seq"),
            P(),
            P(),
        ),
        out_specs=P(None, None, None, "seq"),
        check_vma=False,
    )
```

profile of v0, /device:TPU:0, one launch (start us, length us, event | category | flops | bytes accessed | tf_op | source)
XLA Modules:
  0.0 335.9 jit_solution(9079900889281217494)
XLA Ops:
  0.0 4.6 %copy.174 = bf16[4,2,2048,128]{3,2,1,0:T(8,128)(2,1)} copy(bf16[4,2,2048,128]{3,2,1,0:T(8,128)(2,1)} %param.18) | data formatting | bytes 8388608
  4.6 2.0 copy.175
  6.7 3.9 %fusion.169 = (f32[4,2,32]{2,1,0:T(2,128)S(1)}, f32[4,2,32,2048]{3,2,1,0:T(8,128)S(1)}) fusion(bf16[4,2,2048,128]{3,2,1,0:T(8,128)(2,1)} %copy.174, bf16[3,4,2,32,128]{4,3,2,1,0:T(8,128)(2,1)S(1)} %copy-done.16, pred[4,2048]{1,0:T(4,128)(4,1)S(1)} %get-tuple-element.48), kind=kOutput, calls=%fused_computation.242 | convolution fusion | flops 135790336 | bytes 6366208 | tf_op jit(solution)/shard_map/bhqd,bhkd->bhqk/dot_general | solution.py:19
  10.7 5.9 %fusion.170 = (f32[4,2,32]{2,1,0:T(2,128)S(1)}, f32[4,2,32,2048]{3,2,1,0:T(8,128)S(1)}) fusion(bf16[3,4,2,32,128]{4,3,2,1,0:T(8,128)(2,1)} %param.16, bf16[4,2,2048,128]{3,2,1,0:T(8,128)(2,1)S(1)} %copy-done.2, pred[4,2048]{1,0:T(4,128)(4,1)S(1)} %get-tuple-element.48, f32[4,2,2048]{2,1,0:T(2,128)S(1)} %copy-done.22, bf16[4,2,2048,128]{3,2,1,0:T(8,128)(2,1)} %param.20), kind=kOutput, calls=%fused_computation.243 | convolution fusion | flops 144178944 | bytes 10634240 | tf_op jit(solution)/shard_map/bhqd,bhkd->bhqk/dot_general | solution.py:19
  16.6 0.9 convert_reduce_fusion.5
  17.5 0.4 copy-done.8
  17.9 0.7 all_to_all.104
  18.6 7.3 %all-to-all-start.2 = ((f32[1,8,64]{2,0,1:T(1,128)}), f32[1,8,64]{2,0,1:T(1,128)S(1)}, u32[]{:S(2)}, u32[]{:S(2)}) async-start(f32[1,8,64]{2,0,1:T(1,128)} %all_to_all.104), calls=%async_computation.2 | async-start | bytes 8192 | tf_op jit(solution)/shard_map/all_to_all | solution.py:64
  25.9 0.2 copy.99
  26.1 0.2 fusion.111
  26.4 0.3 fusion.113
  26.6 0.3 fusion.115
  26.9 38.5 %all-reduce = (bf16[16,512]{1,0:T(8,128)(2,1)S(1)}, bf16[16,512]{1,0:T(8,128)(2,1)S(1)}, bf16[16,512]{1,0:T(8,128)(2,1)S(1)}) all-reduce(f32[16,512]{1,0:T(8,128)S(1)} %fusion.111, f32[16,512]{1,0:T(8,128)S(1)} %fusion.115, f32[16,512]{1,0:T(8,128)S(1)} %fusion.113), channel_id=1, replica_groups=mesh['seq'=8,'tp'=4] {'seq'}, use_global_device_ids=true, to_apply=%region_34.35 | all-reduce | flops 24576 | bytes 147456 | tf_op jit(solution)/shard_map/psum | solution.py:119
  66.8 2.5 scatter_fusion
  69.3 10.5 %copy.76 = bf16[4,2,2048,128]{3,1,2,0:T(2,128)(2,1)} copy(bf16[4,2,2048,128]{3,2,1,0:T(8,128)(2,1)} %scatter_fusion) | data formatting | bytes 8388608 | tf_op jit(solution)/shard_map/scatter | solution.py:143
  80.0 2.6 scatter_fusion.2
  82.6 8.5 %fusion.162 = (f32[4,2,32]{2,1,0:T(2,128)S(1)}, f32[4,2,32,2048]{3,2,1,0:T(8,128)}) fusion(bf16[3,4,2,32,128]{4,3,2,1,0:T(8,128)(2,1)S(1)} %copy-done.21, pred[4,2048]{1,0:T(4,128)(4,1)S(1)} %get-tuple-element.48, bf16[4,2,2048,128]{3,1,2,0:T(2,128)(2,1)} %scatter_fusion.2, f32[4,2,2048]{2,1,0:T(2,128)S(1)} %copy-done.23, ...), kind=kOutput, calls=%fused_computation.235 | convolution fusion | flops 144178944 | bytes 10634240 | tf_op jit(solution)/shard_map/bhqd,bhkd->bhqk/dot_general | solution.py:19
  91.1 2.9 fusion.161
  94.0 6.2 %fusion.168 = (f32[4,2,32]{2,1,0:T(2,128)S(1)}, f32[4,2,32,2048]{3,2,1,0:T(8,128)}) fusion(bf16[3,4,2,32,128]{4,3,2,1,0:T(8,128)(2,1)S(1)} %copy-done.21, bf16[4,2,2048,128]{3,2,1,0:T(8,128)(2,1)S(1)} %copy-done.3, pred[4,2048]{1,0:T(4,128)(4,1)S(1)} %get-tuple-element.48, f32[4,2,2048]{2,1,0:T(2,128)S(1)} %copy-done.23, ...), kind=kOutput, calls=%fused_computation.241 | convolution fusion | flops 144178944 | bytes 10634240 | tf_op jit(solution)/shard_map/bhqd,bhkd->bhqk/dot_general | solution.py:19
  100.2 2.8 fusion.167
  103.1 0.9 convolution_bitcast_fusion.1
  104.0 0.6 copy-done.9
  104.7 1.2 copy-done.20
  105.9 4.2 %fusion.66 = f32[1,4,2,32,128]{4,3,2,1,0:T(8,128)S(1)} fusion(bf16[4,2,2048,128]{3,2,1,0:T(8,128)(2,1)S(1)} %copy-done, pred[4,2048]{1,0:T(4,128)(4,1)S(1)} %get-tuple-element.48, f32[4,2,2048]{2,1,0:T(2,128)S(1)} %copy-done.24, bf16[4,2,2048,128]{3,2,1,0:T(8,128)(2,1)S(1)} %copy-done.20, f32[4,2,32,2048]{3,2,1,0:T(8,128)S(1)} %copy-done.9, ...), kind=kOutput, calls=%fused_computation.62 | convolution fusion | flops 144179200 | bytes 10691584 | tf_op jit(solution)/shard_map/bhqk,bhkd->bhqd/dot_general | solution.py:26
  110.2 0.7 pad_maximum_fusion
  110.9 2.5 scatter_fusion.1
  113.4 10.6 %copy.80 = bf16[4,2,2048,128]{3,1,2,0:T(2,128)(2,1)} copy(bf16[4,2,2048,128]{3,2,1,0:T(8,128)(2,1)} %scatter_fusion.1) | data formatting | bytes 8388608 | tf_op jit(solution)/shard_map/scatter | solution.py:146
  124.0 6.0 %fusion.69 = f32[1,4,2,32,128]{4,3,2,1,0:T(8,128)S(1)} fusion(bf16[4,2,2048,128]{3,2,1,0:T(8,128)(2,1)S(1)} %copy-done.1, pred[4,2048]{1,0:T(4,128)(4,1)S(1)} %get-tuple-element.48, f32[4,2,2048]{2,1,0:T(2,128)S(1)} %copy-done.24, bf16[4,2,2048,128]{3,2,1,0:T(8,128)(2,1)} %param.21, f32[4,2,32,2048]{3,2,1,0:T(8,128)S(1)} %copy-done.12, ...), kind=kOutput, calls=%fused_computation.63 | convolution fusion | flops 144179200 | bytes 10699776 | tf_op jit(solution)/shard_map/bhqk,bhkd->bhqd/dot_general | solution.py:26
  130.0 0.9 convolution_bitcast_fusion
  131.0 2.6 scatter_fusion.3
  133.6 7.2 %fusion.72 = f32[1,4,2,32,128]{4,3,2,1,0:T(8,128)S(1)} fusion(pred[4,2048]{1,0:T(4,128)(4,1)S(1)} %get-tuple-element.48, bf16[4,2,2048,128]{3,1,2,0:T(2,128)(2,1)} %scatter_fusion.3, f32[4,2,2048]{2,1,0:T(2,128)S(1)} %copy-done.24, bf16[4,2,2048,128]{3,2,1,0:T(8,128)(2,1)} %param.21, f32[4,2,32,2048]{3,2,1,0:T(8,128)} %get-tuple-element.58, ...), kind=kOutput, calls=%fused_computation.64 | convolution fusion | flops 144179200 | bytes 10699776 | tf_op jit(solution)/shard_map/bhqk,bhkd->bhqd/dot_general | solution.py:26
  140.8 1.9 convert_reduce_fusion.1
  142.7 0.3 copy-done.5
  143.0 1.0 fusion.63
  144.2 0.2 convolution_bitcast_fusion.7
  145.6 0.7 pad_maximum_fusion.2
  146.3 0.7 pad_maximum_fusion.4
  147.1 0.7 all_to_all.101
  147.8 3.2 all-to-all-start.1
  151.0 0.7 all_to_all.109
  151.7 5.7 %all-to-all-done.1 = f32[1,8,64]{2,0,1:T(1,128)S(1)} async-done(((f32[1,8,64]{2,0,1:T(1,128)}), f32[1,8,64]{2,0,1:T(1,128)S(1)}, u32[]{:S(2)}, u32[]{:S(2)}) %all-to-all-start.1) | async-done | bytes 2080 | tf_op jit(solution)/shard_map/all_to_all | solution.py:63
  157.4 3.3 all-to-all-start.4
  161.0 0.7 all_to_all.112
  161.8 0.7 all_to_all.120
  162.5 0.7 all_to_all.117
  163.4 3.8 %all-to-all-done.4 = f32[1,8,64]{2,0,1:T(1,128)S(1)} async-done(((f32[1,8,64]{2,0,1:T(1,128)}), f32[1,8,64]{2,0,1:T(1,128)S(1)}, u32[]{:S(2)}, u32[]{:S(2)}) %all-to-all-start.4) | async-done | bytes 2080 | tf_op jit(solution)/shard_map/all_to_all | solution.py:63
  167.2 3.3 all-to-all-start.5
  170.5 6.4 %all-to-all-done.5 = f32[1,8,64]{2,0,1:T(1,128)S(1)} async-done(((f32[1,8,64]{2,0,1:T(1,128)}), f32[1,8,64]{2,0,1:T(1,128)S(1)}, u32[]{:S(2)}, u32[]{:S(2)}) %all-to-all-start.5) | async-done | bytes 2080 | tf_op jit(solution)/shard_map/all_to_all | solution.py:64
  176.9 3.3 all-to-all-start.8
  180.3 6.3 %all-to-all-done.8 = f32[1,8,64]{2,0,1:T(1,128)S(1)} async-done(((f32[1,8,64]{2,0,1:T(1,128)}), f32[1,8,64]{2,0,1:T(1,128)S(1)}, u32[]{:S(2)}, u32[]{:S(2)}) %all-to-all-start.8) | async-done | bytes 2080 | tf_op jit(solution)/shard_map/all_to_all | solution.py:64
  186.6 3.2 all-to-all-start.7
  189.9 6.3 %all-to-all-done.7 = f32[1,8,64]{2,0,1:T(1,128)S(1)} async-done(((f32[1,8,64]{2,0,1:T(1,128)}), f32[1,8,64]{2,0,1:T(1,128)S(1)}, u32[]{:S(2)}, u32[]{:S(2)}) %all-to-all-start.7) | async-done | bytes 2080 | tf_op jit(solution)/shard_map/all_to_all | solution.py:63
  196.2 3.4 %all-to-all-start = ((f32[1,512,128]{2,0,1:T(1,128)}), f32[1,512,128]{2,0,1:T(1,128)S(1)}, u32[]{:S(2)}, u32[]{:S(2)}) async-start(f32[1,512,128]{2,0,1:T(1,128)} %bitcast.6), calls=%async_computation | async-start | bytes 524288 | tf_op jit(solution)/shard_map/all_to_all | solution.py:65
  199.9 7.9 %all-to-all-done = f32[1,512,128]{2,0,1:T(1,128)S(1)} async-done(((f32[1,512,128]{2,0,1:T(1,128)}), f32[1,512,128]{2,0,1:T(1,128)S(1)}, u32[]{:S(2)}, u32[]{:S(2)}) %all-to-all-start) | async-done | bytes 262176 | tf_op jit(solution)/shard_map/all_to_all | solution.py:65
  207.8 3.4 %all-to-all-start.3 = ((f32[1,512,128]{2,0,1:T(1,128)}), f32[1,512,128]{2,0,1:T(1,128)S(1)}, u32[]{:S(2)}, u32[]{:S(2)}) async-start(f32[1,512,128]{2,0,1:T(1,128)} %bitcast.43), calls=%async_computation.3 | async-start | bytes 524288 | tf_op jit(solution)/shard_map/all_to_all | solution.py:65
  211.5 32.1 %all_gather.9 = bf16[512,128]{1,0:T(8,128)(2,1)S(1)} all-gather(bf16[64,128]{1,0:T(8,128)(2,1)S(1)} %divide_convert_fusion.2), channel_id=1, replica_groups=mesh['seq'=8,'tp'=4] {'seq'}, dimensions={0}, use_global_device_ids=true | all-gather | bytes 147456 | tf_op jit(solution)/shard_map/all_gather | solution.py:83
  243.7 3.0 fusion.171
  246.7 4.5 %all-to-all-start.6 = ((f32[1,512,128]{2,0,1:T(1,128)}), f32[1,512,128]{2,0,1:T(1,128)S(1)}, u32[]{:S(2)}, u32[]{:S(2)}) async-start(f32[1,512,128]{2,0,1:T(1,128)} %bitcast.80), calls=%async_computation.6 | async-start | bytes 524288 | tf_op jit(solution)/shard_map/all_to_all | solution.py:65
  251.5 32.0 %all_gather.10 = bf16[512,128]{1,0:T(8,128)(2,1)S(1)} all-gather(bf16[64,128]{1,0:T(8,128)(2,1)S(1)} %divide_convert_fusion.1), channel_id=1, replica_groups=mesh['seq'=8,'tp'=4] {'seq'}, dimensions={0}, use_global_device_ids=true | all-gather | bytes 147456 | tf_op jit(solution)/shard_map/all_gather | solution.py:83
  283.5 3.0 fusion.172
  286.8 30.5 %all_gather.11 = bf16[512,128]{1,0:T(8,128)(2,1)S(1)} all-gather(bf16[64,128]{1,0:T(8,128)(2,1)S(1)} %divide_convert_fusion), channel_id=1, replica_groups=mesh['seq'=8,'tp'=4] {'seq'}, dimensions={0}, use_global_device_ids=true | all-gather | bytes 147456 | tf_op jit(solution)/shard_map/all_gather | solution.py:83
  317.4 3.0 fusion.173
  320.4 14.8 %all-reduce.3 = (bf16[32,1024]{1,0:T(8,128)(2,1)S(1)}, bf16[32,1024]{1,0:T(8,128)(2,1)S(1)}, bf16[32,1024]{1,0:T(8,128)(2,1)S(1)}) all-reduce(f32[32,1024]{1,0:T(8,128)S(1)} %fusion.173, f32[32,1024]{1,0:T(8,128)S(1)} %fusion.172, f32[32,1024]{1,0:T(8,128)S(1)} %fusion.171), channel_id=1, replica_groups=mesh['seq'=8,'tp'=4] {'tp'}, use_global_device_ids=true, to_apply=%region_42.43 | all-reduce | flops 98304 | bytes 589824 | tf_op jit(solution)/shard_map/psum | solution.py:136
  335.2 0.7 pad_maximum_fusion.6
  (125 shorter events, 4.9 us)
Async XLA Ops:
  0.0 4.6 %copy-start.7 = (bf16[4,2,2048,128]{3,2,1,0:T(8,128)(2,1)S(1)}, bf16[4,2,2048,128]{3,2,1,0:T(8,128)(2,1)}, u32[]{:S(2)}) copy-start(bf16[4,2,2048,128]{3,2,1,0:T(8,128)(2,1)} %param.19) | copy-start | bytes 12582916
  4.6 2.0 copy-start.17
  4.6 2.0 copy-start.18
  4.6 2.1 copy-start.16
  6.7 4.0 %copy-start.2 = (bf16[4,2,2048,128]{3,2,1,0:T(8,128)(2,1)S(1)}, bf16[4,2,2048,128]{3,2,1,0:T(8,128)(2,1)}, u32[]{:S(2)}) copy-start(bf16[4,2,2048,128]{3,2,1,0:T(8,128)(2,1)} %copy.174) | copy-start | bytes 12582916
  6.7 4.0 %copy-start.22 = (f32[4,2,2048]{2,1,0:T(2,128)S(1)}, f32[4,2,2048]{2,1,0:T(2,128)}, u32[]{:S(2)}) copy-start(f32[4,2,2048]{2,1,0:T(2,128)} %param.22) | copy-start | bytes 196612
  16.6 1.3 copy-start.8
  16.6 9.3 %copy-start.14 = (bf16[1024,2,256]{2,1,0:T(2,128)(2,1)S(1)}, bf16[1024,2,256]{2,1,0:T(2,128)(2,1)}, u32[]{:S(2)}) copy-start(bf16[1024,2,256]{2,1,0:T(2,128)(2,1)} %param.14) | copy-start | bytes 3145732
  17.9 8.2 %copy-start.15 = (bf16[3,16,1024]{2,1,0:T(8,128)(2,1)S(1)}, bf16[3,16,1024]{2,1,0:T(8,128)(2,1)}, u32[]{:S(2)}) copy-start(bf16[3,16,1024]{2,1,0:T(8,128)(2,1)} %param.13) | copy-start | bytes 294916
  18.6 129.2 %all-to-all-start.2 = ((f32[1,8,64]{2,0,1:T(1,128)}), f32[1,8,64]{2,0,1:T(1,128)S(1)}, u32[]{:S(2)}, u32[]{:S(2)}) async-start(f32[1,8,64]{2,0,1:T(1,128)} %all_to_all.104), calls=%async_computation.2 | async-start | bytes 8192 | tf_op jit(solution)/shard_map/all_to_all | solution.py:64
  26.1 39.5 %copy-start.21 = (bf16[3,4,2,32,128]{4,3,2,1,0:T(8,128)(2,1)S(1)}, bf16[3,4,2,32,128]{4,3,2,1,0:T(8,128)(2,1)}, u32[]{:S(2)}) copy-start(bf16[3,4,2,32,128]{4,3,2,1,0:T(8,128)(2,1)} %param.16) | copy-start | bytes 589828
  69.3 13.3 %copy-start.23 = (f32[4,2,2048]{2,1,0:T(2,128)S(1)}, f32[4,2,2048]{2,1,0:T(2,128)}, u32[]{:S(2)}) copy-start(f32[4,2,2048]{2,1,0:T(2,128)} %param.22) | copy-start | bytes 196612
  82.6 8.5 %copy-start.6 = (bf16[4,2,2048,128]{3,1,2,0:T(2,128)(2,1)S(1)}, bf16[4,2,2048,128]{3,1,2,0:T(2,128)(2,1)}, u32[]{:S(2)}) copy-start(bf16[4,2,2048,128]{3,1,2,0:T(2,128)(2,1)} %scatter_fusion.2) | copy-start | bytes 12582916
  82.6 11.4 %copy-start.19 = (bf16[4,2,2048,128]{3,2,1,0:T(8,128)(2,1)S(1)}, bf16[4,2,2048,128]{3,2,1,0:T(8,128)(2,1)}, u32[]{:S(2)}) copy-start(bf16[4,2,2048,128]{3,2,1,0:T(8,128)(2,1)} %param.20) | copy-start | bytes 12582916
  91.1 2.9 copy-start.3
  100.2 2.8 copy-start
  103.1 1.6 copy-start.9
  103.1 2.8 copy-start.20
  103.1 2.8 copy-start.24
  113.4 10.6 %copy-start.1 = (bf16[4,2,2048,128]{3,2,1,0:T(8,128)(2,1)S(1)}, bf16[4,2,2048,128]{3,2,1,0:T(8,128)(2,1)}, u32[]{:S(2)}) copy-start(bf16[4,2,2048,128]{3,2,1,0:T(8,128)(2,1)} %scatter_fusion.1) | copy-start | bytes 12582916
  113.4 10.6 %copy-start.12 = (f32[4,2,32,2048]{3,2,1,0:T(8,128)S(1)}, f32[4,2,32,2048]{3,2,1,0:T(8,128)}, u32[]{:S(2)}) copy-start(f32[4,2,32,2048]{3,2,1,0:T(8,128)} %get-tuple-element.70) | copy-start | bytes 6291460
  124.0 6.0 %copy-start.4 = (f32[4,2,32,2048]{3,2,1,0:T(8,128)S(1)}, f32[4,2,32,2048]{3,2,1,0:T(8,128)}, u32[]{:S(2)}) copy-start(f32[4,2,32,2048]{3,2,1,0:T(8,128)} %get-tuple-element.68) | copy-start | bytes 6291460
  133.6 7.2 %copy-start.10 = (f32[4,2,32,2048]{3,2,1,0:T(8,128)S(1)}, f32[4,2,32,2048]{3,2,1,0:T(8,128)}, u32[]{:S(2)}) copy-start(f32[4,2,32,2048]{3,2,1,0:T(8,128)} %get-tuple-element.56) | copy-start | bytes 6291460
  133.6 7.2 %copy-start.11 = (f32[4,2,32,2048]{3,2,1,0:T(8,128)S(1)}, f32[4,2,32,2048]{3,2,1,0:T(8,128)}, u32[]{:S(2)}) copy-start(f32[4,2,32,2048]{3,2,1,0:T(8,128)} %get-tuple-element.58) | copy-start | bytes 6291460
  133.6 7.2 %copy-start.13 = (f32[4,2,32,2048]{3,2,1,0:T(8,128)S(1)}, f32[4,2,32,2048]{3,2,1,0:T(8,128)}, u32[]{:S(2)}) copy-start(f32[4,2,32,2048]{3,2,1,0:T(8,128)} %get-tuple-element.70) | copy-start | bytes 6291460
  140.8 2.2 copy-start.5
  147.8 9.7 %all-to-all-start.1 = ((f32[1,8,64]{2,0,1:T(1,128)}), f32[1,8,64]{2,0,1:T(1,128)S(1)}, u32[]{:S(2)}, u32[]{:S(2)}) async-start(f32[1,8,64]{2,0,1:T(1,128)} %all_to_all.101), calls=%async_computation.1 | async-start | bytes 8192 | tf_op jit(solution)/shard_map/all_to_all | solution.py:63
  157.4 9.8 %all-to-all-start.4 = ((f32[1,8,64]{2,0,1:T(1,128)}), f32[1,8,64]{2,0,1:T(1,128)S(1)}, u32[]{:S(2)}, u32[]{:S(2)}) async-start(f32[1,8,64]{2,0,1:T(1,128)} %all_to_all.109), calls=%async_computation.4 | async-start | bytes 8192 | tf_op jit(solution)/shard_map/all_to_all | solution.py:63
  167.2 9.7 %all-to-all-start.5 = ((f32[1,8,64]{2,0,1:T(1,128)}), f32[1,8,64]{2,0,1:T(1,128)S(1)}, u32[]{:S(2)}, u32[]{:S(2)}) async-start(f32[1,8,64]{2,0,1:T(1,128)} %all_to_all.112), calls=%async_computation.5 | async-start | bytes 8192 | tf_op jit(solution)/shard_map/all_to_all | solution.py:64
  176.9 9.7 %all-to-all-start.8 = ((f32[1,8,64]{2,0,1:T(1,128)}), f32[1,8,64]{2,0,1:T(1,128)S(1)}, u32[]{:S(2)}, u32[]{:S(2)}) async-start(f32[1,8,64]{2,0,1:T(1,128)} %all_to_all.120), calls=%async_computation.8 | async-start | bytes 8192 | tf_op jit(solution)/shard_map/all_to_all | solution.py:64
  186.6 9.7 %all-to-all-start.7 = ((f32[1,8,64]{2,0,1:T(1,128)}), f32[1,8,64]{2,0,1:T(1,128)S(1)}, u32[]{:S(2)}, u32[]{:S(2)}) async-start(f32[1,8,64]{2,0,1:T(1,128)} %all_to_all.117), calls=%async_computation.7 | async-start | bytes 8192 | tf_op jit(solution)/shard_map/all_to_all | solution.py:63
  196.2 11.6 %all-to-all-start = ((f32[1,512,128]{2,0,1:T(1,128)}), f32[1,512,128]{2,0,1:T(1,128)S(1)}, u32[]{:S(2)}, u32[]{:S(2)}) async-start(f32[1,512,128]{2,0,1:T(1,128)} %bitcast.6), calls=%async_computation | async-start | bytes 524288 | tf_op jit(solution)/shard_map/all_to_all | solution.py:65
  207.8 38.8 %all-to-all-start.3 = ((f32[1,512,128]{2,0,1:T(1,128)}), f32[1,512,128]{2,0,1:T(1,128)S(1)}, u32[]{:S(2)}, u32[]{:S(2)}) async-start(f32[1,512,128]{2,0,1:T(1,128)} %bitcast.43), calls=%async_computation.3 | async-start | bytes 524288 | tf_op jit(solution)/shard_map/all_to_all | solution.py:65
  246.7 39.8 %all-to-all-start.6 = ((f32[1,512,128]{2,0,1:T(1,128)}), f32[1,512,128]{2,0,1:T(1,128)S(1)}, u32[]{:S(2)}, u32[]{:S(2)}) async-start(f32[1,512,128]{2,0,1:T(1,128)} %bitcast.80), calls=%async_computation.6 | async-start | bytes 524288 | tf_op jit(solution)/shard_map/all_to_all | solution.py:65
where the time goes:
time: 337 us; the launch traced here: 336 us
  blocking collectives  148 us (44%)
  matrix products  62.7 us (19%)
  local copies, waits for them, and re-layouts  45.8 us (14%)
  waiting for transfers between devices  36.6 us (11%)
  starting transfers between devices  35 us (10%)
  other arithmetic  7.3 us (2%)
    all_gather x3, blocking collectives, spread_merge(): gathered = lax.all_gather(merged, 'seq', axis=0, tiled=True)  94.5 us
    psum x1, blocking collectives, per_device(): lax.psum(partial_kv, 'seq').astype(jnp.bfloat16)  38.5 us
    dot_general x12, matrix products, attend(): jnp.einsum('bhqd,bhkd->bhqk', queries, keys, preferred_element_type=jnp.f...  31.3 us
    dot_general x12, matrix products, attend(): jnp.einsum('bhqk,bhkd->bhqd', weights, values, preferred_element_type=jnp...  21.6 us
    all_to_all x3, waiting for transfers between devices, spread_merge(): lax.all_to_all(maxima, 'seq', split_axis=1, concat_axis=0, tiled=True)  15.9 us
    scatter x3, local copies, waits for them, and re-layouts, per_device(): values_cache.at[batch_rows, :, targets, :]  15.7 us
    scatter x3, local copies, waits for them, and re-layouts, per_device(): keys_cache.at[batch_rows, :, targets, :]  15.6 us
    psum x1, blocking collectives, per_device(): summed = lax.psum(projected, 'tp')  14.8 us
  transfers between devices with their start and end apart: 9, of which 6 were waited for; matrix products, arithmetic and copies ran while one was open for 26% of the time, Pallas kernels for 0%

commit v1 on v0

--- a/solution.py
+++ b/solution.py
@@ -115,8 +115,13 @@
     results = []
     for turn_index in range(ROUNDS):
         partial_kv = jnp.dot(hidden_new[turn_index], flat_kv, preferred_element_type=jnp.float32)
+
+        def create_wires_on_mesh(a0):
+            reached = lax.all_gather(a0, axis_name="seq")
+            return jnp.sum(reached, 0)
+
         fresh_rows = (
-            lax.psum(partial_kv, "seq")
+            create_wires_on_mesh(partial_kv)
             .astype(jnp.bfloat16)
             .reshape(batch_size, R, head_count, 2, head_width)
         )

time: 337 us -> 424 us (1.26)
  blocking collectives: 148 us -> 201 us
  local copies, waits for them, and re-layouts: 45.8 us -> 73.7 us
    all_gather x0 -> x3, blocking collectives: none -> 92.8 us  [create_wires_on_mesh(): reached = lax.all_gather(a0, axis_name='seq')]
    psum x1 -> x0, blocking collectives: 38.5 us -> none  [per_device(): lax.psum(partial_kv, 'seq').astype(jnp.bfloat16)]
    scatter x3, local copies, waits for them, and re-layouts: 15.6 us -> 40.8 us  [per_device(): keys_cache.at[batch_rows, :, targets, :]]
    unnamed x53 -> x59, local copies, waits for them, and re-layouts: 9.41 us -> 11.4 us
  transfers between devices with their start and end apart: 9 -> 9, of which waited for: 6 -> 6; matrix products, arithmetic and copies ran while one was open for 26% -> 27% of each run, Pallas kernels for 0% -> 0%
where the time goes in v1:
time: 424 us; the launch traced here: 422 us
  blocking collectives  201 us (47%)
  local copies, waits for them, and re-layouts  73.7 us (17%)
  matrix products  64.6 us (15%)
  starting transfers between devices  37.9 us (9%)
  waiting for transfers between devices  36.6 us (9%)
  other arithmetic  7.38 us (2%)
    all_gather x3, blocking collectives, spread_merge(): gathered = lax.all_gather(merged, 'seq', axis=0, tiled=True)  93.6 us
    all_gather x3, blocking collectives, create_wires_on_mesh(): reached = lax.all_gather(a0, axis_name='seq')  92.8 us
    scatter x3, local copies, waits for them, and re-layouts, per_device(): keys_cache.at[batch_rows, :, targets, :]  40.8 us
    dot_general x12, matrix products, attend(): jnp.einsum('bhqd,bhkd->bhqk', queries, keys, preferred_element_type=jnp.f...  35.1 us
    dot_general x12, matrix products, attend(): jnp.einsum('bhqk,bhkd->bhqd', weights, values, preferred_element_type=jnp...  19.8 us
    all_to_all x3, waiting for transfers between devices, spread_merge(): lax.all_to_all(maxima, 'seq', split_axis=1, concat_axis=0, tiled=True)  16 us
    scatter x3, local copies, waits for them, and re-layouts, per_device(): values_cache.at[batch_rows, :, targets, :]  16 us
    psum x1, blocking collectives, per_device(): summed = lax.psum(projected, 'tp')  14.9 us
  transfers between devices with their start and end apart: 9, of which 6 were waited for; matrix products, arithmetic and copies ran while one was open for 27% of the time, Pallas kernels for 0%

profile of v1, /device:TPU:0, one launch (start us, length us, event | category | flops | bytes accessed | tf_op | source)
XLA Modules:
  0.0 422.1 jit_solution(213200153600396702)
XLA Ops:
  0.0 4.6 %copy.168 = bf16[4,2,2048,128]{3,2,1,0:T(8,128)(2,1)} copy(bf16[4,2,2048,128]{3,2,1,0:T(8,128)(2,1)} %param.18) | data formatting | bytes 8388608
  4.6 1.9 copy.169
  6.7 4.0 fusion.169
  10.7 5.9 %fusion.170 = (f32[4,2,32]{2,1,0:T(2,128)S(1)}, f32[4,2,32,2048]{3,2,1,0:T(8,128)S(1)}) fusion(bf16[3,4,2,32,128]{4,3,2,1,0:T(8,128)(2,1)} %param.16, bf16[4,2,2048,128]{3,2,1,0:T(8,128)(2,1)S(1)} %copy-done.2, pred[4,2048]{1,0:T(4,128)(4,1)S(1)} %get-tuple-element.45, f32[4,2,2048]{2,1,0:T(2,128)S(1)} %copy-done.24, bf16[4,2,2048,128]{3,2,1,0:T(8,128)(2,1)} %param.20), kind=kOutput, calls=%fused_computation.243 | convolution fusion | flops 144178944 | bytes 10634240 | tf_op jit(solution)/shard_map/bhqd,bhkd->bhqk/dot_general | solution.py:19
  16.6 0.9 convert_reduce_fusion.5
  17.6 0.4 copy-done.8
  18.0 0.7 all_to_all.104
  18.7 7.3 %all-to-all-start.2 = ((f32[1,8,64]{2,0,1:T(1,128)}), f32[1,8,64]{2,0,1:T(1,128)S(1)}, u32[]{:S(2)}, u32[]{:S(2)}) async-start(f32[1,8,64]{2,0,1:T(1,128)} %all_to_all.104), calls=%async_computation.2 | async-start | bytes 8192 | tf_op jit(solution)/shard_map/all_to_all | solution.py:64
  26.0 0.5 slice_bitcast_fusion
  27.5 31.3 %all-gather = f32[128,512]{1,0:T(8,128)S(1)} all-gather(f32[16,512]{1,0:T(8,128)S(1)} %fusion.115), channel_id=2, replica_groups=mesh['seq'=8,'tp'=4] {'seq'}, dimensions={0}, use_global_device_ids=true | all-gather | bytes 294912 | tf_op jit(solution)/shard_map/all_gather | solution.py:120
  59.2 30.7 %all-gather.1 = f32[128,512]{1,0:T(8,128)S(1)} all-gather(f32[16,512]{1,0:T(8,128)S(1)} %fusion.113), channel_id=3, replica_groups=mesh['seq'=8,'tp'=4] {'seq'}, dimensions={0}, use_global_device_ids=true | all-gather | bytes 294912 | tf_op jit(solution)/shard_map/all_gather | solution.py:120
  90.4 30.7 %all-gather.2 = f32[128,512]{1,0:T(8,128)S(1)} all-gather(f32[16,512]{1,0:T(8,128)S(1)} %fusion.111), channel_id=4, replica_groups=mesh['seq'=8,'tp'=4] {'seq'}, dimensions={0}, use_global_device_ids=true | all-gather | bytes 294912 | tf_op jit(solution)/shard_map/all_gather | solution.py:120
  123.2 2.7 scatter_fusion
  125.9 5.2 %fusion.167 = (f32[4,2,32]{2,1,0:T(2,128)S(1)}, f32[4,2,32,2048]{3,2,1,0:T(8,128)}) fusion(bf16[4,2,2048,128]{3,2,1,0:T(8,128)(2,1)} %scatter_fusion, bf16[3,4,2,32,128]{4,3,2,1,0:T(8,128)(2,1)S(1)} %copy-done.16, pred[4,2048]{1,0:T(4,128)(4,1)S(1)} %get-tuple-element.43), kind=kOutput, calls=%fused_computation.240 | convolution fusion | flops 135790336 | bytes 6366208 | tf_op jit(solution)/shard_map/bhqd,bhkd->bhqk/dot_general | solution.py:19
  131.1 6.8 %fusion.168 = (f32[4,2,32]{2,1,0:T(2,128)S(1)}, f32[4,2,32,2048]{3,2,1,0:T(8,128)}) fusion(bf16[3,4,2,32,128]{4,3,2,1,0:T(8,128)(2,1)S(1)} %copy-done.23, bf16[4,2,2048,128]{3,2,1,0:T(8,128)(2,1)S(1)} %copy-done.3, pred[4,2048]{1,0:T(4,128)(4,1)S(1)} %get-tuple-element.45, f32[4,2,2048]{2,1,0:T(2,128)S(1)} %copy-done.25, ...), kind=kOutput, calls=%fused_computation.241 | convolution fusion | flops 144178944 | bytes 10634240 | tf_op jit(solution)/shard_map/bhqd,bhkd->bhqk/dot_general | solution.py:19
  137.8 35.4 %copy.70 = bf16[4,2,2048,128]{3,1,2,0:T(2,128)(2,1)} copy(bf16[4,2,2048,128]{3,2,1,0:T(8,128)(2,1)S(1)} %copy-done.3) | data formatting | bytes 8388608 | tf_op jit(solution)/shard_map/scatter | solution.py:148
  173.4 2.7 scatter_fusion.2
  176.1 5.2 %fusion.161 = (f32[4,2,32]{2,1,0:T(2,128)S(1)}, f32[4,2,32,2048]{3,2,1,0:T(8,128)}) fusion(bf16[3,4,2,32,128]{4,3,2,1,0:T(8,128)(2,1)S(1)} %copy-done.16, bf16[4,2,2048,128]{3,1,2,0:T(2,128)(2,1)} %scatter_fusion.2, pred[4,2048]{1,0:T(4,128)(4,1)S(1)} %get-tuple-element.44), kind=kOutput, calls=%fused_computation.234 | convolution fusion | flops 135790336 | bytes 6366208 | tf_op jit(solution)/shard_map/bhqd,bhkd->bhqk/dot_general | solution.py:19
  181.3 7.0 %fusion.162 = (f32[4,2,32]{2,1,0:T(2,128)S(1)}, f32[4,2,32,2048]{3,2,1,0:T(8,128)}) fusion(bf16[3,4,2,32,128]{4,3,2,1,0:T(8,128)(2,1)S(1)} %copy-done.23, pred[4,2048]{1,0:T(4,128)(4,1)S(1)} %get-tuple-element.45, bf16[4,2,2048,128]{3,1,2,0:T(2,128)(2,1)S(1)} %copy-done.5, f32[4,2,2048]{2,1,0:T(2,128)S(1)} %copy-done.25, ...), kind=kOutput, calls=%fused_computation.235 | convolution fusion | flops 144178944 | bytes 10634240 | tf_op jit(solution)/shard_map/bhqd,bhkd->bhqk/dot_general | solution.py:19
  188.4 0.9 convolution_bitcast_fusion.1
  189.3 0.6 copy-done.9
  190.0 1.2 copy-done.20
  191.2 4.2 fusion.66
  195.4 2.7 scatter_fusion.1
  198.1 10.6 %copy.74 = bf16[4,2,2048,128]{3,1,2,0:T(2,128)(2,1)} copy(bf16[4,2,2048,128]{3,2,1,0:T(8,128)(2,1)} %scatter_fusion.1) | data formatting | bytes 8388608 | tf_op jit(solution)/shard_map/scatter | solution.py:151
  208.8 0.9 convolution_bitcast_fusion
  209.7 0.6 copy-done.10
  210.3 1.2 copy-done.21
  211.6 4.2 fusion.69
  215.8 2.7 scatter_fusion.3
  218.4 7.3 %fusion.72 = f32[1,4,2,32,128]{4,3,2,1,0:T(8,128)S(1)} fusion(pred[4,2048]{1,0:T(4,128)(4,1)S(1)} %get-tuple-element.45, bf16[4,2,2048,128]{3,1,2,0:T(2,128)(2,1)} %scatter_fusion.3, f32[4,2,2048]{2,1,0:T(2,128)} %param.23, bf16[4,2,2048,128]{3,2,1,0:T(8,128)(2,1)} %param.21, f32[4,2,32,2048]{3,2,1,0:T(8,128)} %get-tuple-element.55, ...), kind=kOutput, calls=%fused_computation.64 | convolution fusion | flops 144179200 | bytes 10699776 | tf_op jit(solution)/shard_map/bhqk,bhkd->bhqd/dot_general | solution.py:26
  225.7 1.9 convert_reduce_fusion.1
  227.6 0.3 copy-done.6
  227.9 1.0 fusion.63
  228.9 0.7 pad_maximum_fusion
  229.8 0.7 pad_maximum_fusion.4
  230.5 0.7 pad_maximum_fusion.2
  231.2 0.7 all_to_all.101
  231.9 6.0 %all-to-all-start.1 = ((f32[1,8,64]{2,0,1:T(1,128)}), f32[1,8,64]{2,0,1:T(1,128)S(1)}, u32[]{:S(2)}, u32[]{:S(2)}) async-start(f32[1,8,64]{2,0,1:T(1,128)} %all_to_all.101), calls=%async_computation.1 | async-start | bytes 8192 | tf_op jit(solution)/shard_map/all_to_all | solution.py:63
  238.0 0.7 all_to_all.109
  238.6 5.8 %all-to-all-done.1 = f32[1,8,64]{2,0,1:T(1,128)S(1)} async-done(((f32[1,8,64]{2,0,1:T(1,128)}), f32[1,8,64]{2,0,1:T(1,128)S(1)}, u32[]{:S(2)}, u32[]{:S(2)}) %all-to-all-start.1) | async-done | bytes 2080 | tf_op jit(solution)/shard_map/all_to_all | solution.py:63
  244.4 3.3 all-to-all-start.4
  247.8 0.7 all_to_all.117
  248.4 5.7 %all-to-all-done.4 = f32[1,8,64]{2,0,1:T(1,128)S(1)} async-done(((f32[1,8,64]{2,0,1:T(1,128)}), f32[1,8,64]{2,0,1:T(1,128)S(1)}, u32[]{:S(2)}, u32[]{:S(2)}) %all-to-all-start.4) | async-done | bytes 2080 | tf_op jit(solution)/shard_map/all_to_all | solution.py:63
  254.1 3.3 all-to-all-start.7
  258.0 0.7 all_to_all.120
  258.6 0.7 all_to_all.112
  259.3 4.5 %all-to-all-done.7 = f32[1,8,64]{2,0,1:T(1,128)S(1)} async-done(((f32[1,8,64]{2,0,1:T(1,128)}), f32[1,8,64]{2,0,1:T(1,128)S(1)}, u32[]{:S(2)}, u32[]{:S(2)}) %all-to-all-start.7) | async-done | bytes 2080 | tf_op jit(solution)/shard_map/all_to_all | solution.py:63
  263.9 3.2 all-to-all-start.5
  267.2 6.4 %all-to-all-done.5 = f32[1,8,64]{2,0,1:T(1,128)S(1)} async-done(((f32[1,8,64]{2,0,1:T(1,128)}), f32[1,8,64]{2,0,1:T(1,128)S(1)}, u32[]{:S(2)}, u32[]{:S(2)}) %all-to-all-start.5) | async-done | bytes 2080 | tf_op jit(solution)/shard_map/all_to_all | solution.py:64
  273.5 3.3 all-to-all-start.8
  276.9 6.3 %all-to-all-done.8 = f32[1,8,64]{2,0,1:T(1,128)S(1)} async-done(((f32[1,8,64]{2,0,1:T(1,128)}), f32[1,8,64]{2,0,1:T(1,128)S(1)}, u32[]{:S(2)}, u32[]{:S(2)}) %all-to-all-start.8) | async-done | bytes 2080 | tf_op jit(solution)/shard_map/all_to_all | solution.py:64
  283.2 3.4 all-to-all-start.6
  286.8 7.9 %all-to-all-done.6 = f32[1,512,128]{2,0,1:T(1,128)S(1)} async-done(((f32[1,512,128]{2,0,1:T(1,128)}), f32[1,512,128]{2,0,1:T(1,128)S(1)}, u32[]{:S(2)}, u32[]{:S(2)}) %all-to-all-start.6) | async-done | bytes 262176 | tf_op jit(solution)/shard_map/all_to_all | solution.py:65
  294.8 3.4 all-to-all-start.3
  298.5 32.0 %all_gather.35 = bf16[512,128]{1,0:T(8,128)(2,1)S(1)} all-gather(bf16[64,128]{1,0:T(8,128)(2,1)S(1)} %divide_convert_fusion), channel_id=1, replica_groups=mesh['seq'=8,'tp'=4] {'seq'}, dimensions={0}, use_global_device_ids=true | all-gather | bytes 147456 | tf_op jit(solution)/shard_map/all_gather | solution.py:83
  330.6 4.6 %all-to-all-start = ((f32[1,512,128]{2,0,1:T(1,128)}), f32[1,512,128]{2,0,1:T(1,128)S(1)}, u32[]{:S(2)}, u32[]{:S(2)}) async-start(f32[1,512,128]{2,0,1:T(1,128)} %bitcast.6), calls=%async_computation | async-start | bytes 524288 | tf_op jit(solution)/shard_map/all_to_all | solution.py:65
  335.3 3.0 fusion.173
  338.4 31.1 %all_gather.32 = bf16[512,128]{1,0:T(8,128)(2,1)S(1)} all-gather(bf16[64,128]{1,0:T(8,128)(2,1)S(1)} %divide_convert_fusion.1), channel_id=1, replica_groups=mesh['seq'=8,'tp'=4] {'seq'}, dimensions={0}, use_global_device_ids=true | all-gather | bytes 147456 | tf_op jit(solution)/shard_map/all_gather | solution.py:83
  369.6 3.0 fusion.172
  372.9 30.5 %all_gather.29 = bf16[512,128]{1,0:T(8,128)(2,1)S(1)} all-gather(bf16[64,128]{1,0:T(8,128)(2,1)S(1)} %divide_convert_fusion.2), channel_id=1, replica_groups=mesh['seq'=8,'tp'=4] {'seq'}, dimensions={0}, use_global_device_ids=true | all-gather | bytes 147456 | tf_op jit(solution)/shard_map/all_gather | solution.py:83
  403.5 3.0 fusion.171
  406.5 14.9 %all-reduce.2 = (bf16[32,1024]{1,0:T(8,128)(2,1)S(1)}, bf16[32,1024]{1,0:T(8,128)(2,1)S(1)}, bf16[32,1024]{1,0:T(8,128)(2,1)S(1)}) all-reduce(f32[32,1024]{1,0:T(8,128)S(1)} %fusion.173, f32[32,1024]{1,0:T(8,128)S(1)} %fusion.172, f32[32,1024]{1,0:T(8,128)S(1)} %fusion.171), channel_id=1, replica_groups=mesh['seq'=8,'tp'=4] {'tp'}, use_global_device_ids=true, to_apply=%region_42.43 | all-reduce | flops 98304 | bytes 589824 | tf_op jit(solution)/shard_map/psum | solution.py:141
  421.4 0.7 pad_maximum_fusion.6
  (136 shorter events, 6.2 us)
Async XLA Ops:
  0.0 4.6 %copy-start.7 = (bf16[4,2,2048,128]{3,2,1,0:T(8,128)(2,1)S(1)}, bf16[4,2,2048,128]{3,2,1,0:T(8,128)(2,1)}, u32[]{:S(2)}) copy-start(bf16[4,2,2048,128]{3,2,1,0:T(8,128)(2,1)} %param.19) | copy-start | bytes 12582916
  4.6 1.9 copy-start.17
  4.6 1.9 copy-start.18
  4.6 2.1 copy-start.16
  6.7 4.0 copy-start.2
  6.7 4.0 copy-start.24
  16.6 1.4 copy-start.8
  16.6 9.8 %copy-start.14 = (bf16[1024,2,256]{2,1,0:T(2,128)(2,1)S(1)}, bf16[1024,2,256]{2,1,0:T(2,128)(2,1)}, u32[]{:S(2)}) copy-start(bf16[1024,2,256]{2,1,0:T(2,128)(2,1)} %param.14) | copy-start | bytes 3145732
  18.0 8.7 %copy-start.15 = (bf16[3,16,1024]{2,1,0:T(8,128)(2,1)S(1)}, bf16[3,16,1024]{2,1,0:T(8,128)(2,1)}, u32[]{:S(2)}) copy-start(bf16[3,16,1024]{2,1,0:T(8,128)(2,1)} %param.13) | copy-start | bytes 294916
  18.7 213.2 %all-to-all-start.2 = ((f32[1,8,64]{2,0,1:T(1,128)}), f32[1,8,64]{2,0,1:T(1,128)S(1)}, u32[]{:S(2)}, u32[]{:S(2)}) async-start(f32[1,8,64]{2,0,1:T(1,128)} %all_to_all.104), calls=%async_computation.2 | async-start | bytes 8192 | tf_op jit(solution)/shard_map/all_to_all | solution.py:64
  26.7 32.3 %copy-start.22 = (bf16[3,4,2,32,128]{4,3,2,1,0:T(8,128)(2,1)S(1)}, bf16[3,4,2,32,128]{4,3,2,1,0:T(8,128)(2,1)}, u32[]{:S(2)}) copy-start(bf16[3,4,2,32,128]{4,3,2,1,0:T(8,128)(2,1)} %param.16) | copy-start | bytes 589828
  27.4 95.6 %copy-start.19 = (s32[4]{0:T(128)S(1)}, s32[4]{0:T(128)}, u32[]{:S(2)}) copy-start(s32[4]{0:T(128)} %get-tuple-element.47) | copy-start | bytes 52
  125.9 5.2 %copy-start.3 = (bf16[4,2,2048,128]{3,2,1,0:T(8,128)(2,1)S(1)}, bf16[4,2,2048,128]{3,2,1,0:T(8,128)(2,1)}, u32[]{:S(2)}) copy-start(bf16[4,2,2048,128]{3,2,1,0:T(8,128)(2,1)} %scatter_fusion) | copy-start | bytes 12582916
  125.9 5.2 %copy-start.23 = (bf16[3,4,2,32,128]{4,3,2,1,0:T(8,128)(2,1)S(1)}, bf16[3,4,2,32,128]{4,3,2,1,0:T(8,128)(2,1)}, u32[]{:S(2)}) copy-start(bf16[3,4,2,32,128]{4,3,2,1,0:T(8,128)(2,1)} %param.16) | copy-start | bytes 589828
  125.9 5.2 %copy-start.25 = (f32[4,2,2048]{2,1,0:T(2,128)S(1)}, f32[4,2,2048]{2,1,0:T(2,128)}, u32[]{:S(2)}) copy-start(f32[4,2,2048]{2,1,0:T(2,128)} %param.22) | copy-start | bytes 196612
  176.1 5.2 %copy-start.5 = (bf16[4,2,2048,128]{3,1,2,0:T(2,128)(2,1)S(1)}, bf16[4,2,2048,128]{3,1,2,0:T(2,128)(2,1)}, u32[]{:S(2)}) copy-start(bf16[4,2,2048,128]{3,1,2,0:T(2,128)(2,1)} %scatter_fusion.2) | copy-start | bytes 12582916
  181.3 7.0 %copy-start = (bf16[4,2,2048,128]{3,2,1,0:T(8,128)(2,1)S(1)}, bf16[4,2,2048,128]{3,2,1,0:T(8,128)(2,1)}, u32[]{:S(2)}) copy-start(bf16[4,2,2048,128]{3,2,1,0:T(8,128)(2,1)} %copy.169) | copy-start | bytes 12582916
  188.4 1.6 copy-start.9
  188.4 2.8 copy-start.20
  188.4 2.8 copy-start.26
  198.1 10.6 %copy-start.1 = (bf16[4,2,2048,128]{3,2,1,0:T(8,128)(2,1)S(1)}, bf16[4,2,2048,128]{3,2,1,0:T(8,128)(2,1)}, u32[]{:S(2)}) copy-start(bf16[4,2,2048,128]{3,2,1,0:T(8,128)(2,1)} %scatter_fusion.1) | copy-start | bytes 12582916
  198.1 10.6 %copy-start.4 = (f32[4,2,32,2048]{3,2,1,0:T(8,128)S(1)}, f32[4,2,32,2048]{3,2,1,0:T(8,128)}, u32[]{:S(2)}) copy-start(f32[4,2,32,2048]{3,2,1,0:T(8,128)} %get-tuple-element.65) | copy-start | bytes 6291460
  208.7 1.6 copy-start.10
  208.7 2.8 copy-start.21
  208.7 2.8 copy-start.27
  218.4 7.3 %copy-start.11 = (f32[4,2,32,2048]{3,2,1,0:T(8,128)S(1)}, f32[4,2,32,2048]{3,2,1,0:T(8,128)}, u32[]{:S(2)}) copy-start(f32[4,2,32,2048]{3,2,1,0:T(8,128)} %get-tuple-element.67) | copy-start | bytes 6291460
  218.4 7.3 %copy-start.12 = (f32[4,2,32,2048]{3,2,1,0:T(8,128)S(1)}, f32[4,2,32,2048]{3,2,1,0:T(8,128)}, u32[]{:S(2)}) copy-start(f32[4,2,32,2048]{3,2,1,0:T(8,128)} %get-tuple-element.53) | copy-start | bytes 6291460
  218.4 7.3 %copy-start.13 = (f32[4,2,32,2048]{3,2,1,0:T(8,128)S(1)}, f32[4,2,32,2048]{3,2,1,0:T(8,128)}, u32[]{:S(2)}) copy-start(f32[4,2,32,2048]{3,2,1,0:T(8,128)} %get-tuple-element.55) | copy-start | bytes 6291460
  225.7 2.2 copy-start.6
  231.9 12.5 %all-to-all-start.1 = ((f32[1,8,64]{2,0,1:T(1,128)}), f32[1,8,64]{2,0,1:T(1,128)S(1)}, u32[]{:S(2)}, u32[]{:S(2)}) async-start(f32[1,8,64]{2,0,1:T(1,128)} %all_to_all.101), calls=%async_computation.1 | async-start | bytes 8192 | tf_op jit(solution)/shard_map/all_to_all | solution.py:63
  244.4 9.7 %all-to-all-start.4 = ((f32[1,8,64]{2,0,1:T(1,128)}), f32[1,8,64]{2,0,1:T(1,128)S(1)}, u32[]{:S(2)}, u32[]{:S(2)}) async-start(f32[1,8,64]{2,0,1:T(1,128)} %all_to_all.109), calls=%async_computation.4 | async-start | bytes 8192 | tf_op jit(solution)/shard_map/all_to_all | solution.py:63
  254.1 9.8 %all-to-all-start.7 = ((f32[1,8,64]{2,0,1:T(1,128)}), f32[1,8,64]{2,0,1:T(1,128)S(1)}, u32[]{:S(2)}, u32[]{:S(2)}) async-start(f32[1,8,64]{2,0,1:T(1,128)} %all_to_all.117), calls=%async_computation.7 | async-start | bytes 8192 | tf_op jit(solution)/shard_map/all_to_all | solution.py:63
  263.9 9.7 %all-to-all-start.5 = ((f32[1,8,64]{2,0,1:T(1,128)}), f32[1,8,64]{2,0,1:T(1,128)S(1)}, u32[]{:S(2)}, u32[]{:S(2)}) async-start(f32[1,8,64]{2,0,1:T(1,128)} %all_to_all.112), calls=%async_computation.5 | async-start | bytes 8192 | tf_op jit(solution)/shard_map/all_to_all | solution.py:64
  273.5 9.7 %all-to-all-start.8 = ((f32[1,8,64]{2,0,1:T(1,128)}), f32[1,8,64]{2,0,1:T(1,128)S(1)}, u32[]{:S(2)}, u32[]{:S(2)}) async-start(f32[1,8,64]{2,0,1:T(1,128)} %all_to_all.120), calls=%async_computation.8 | async-start | bytes 8192 | tf_op jit(solution)/shard_map/all_to_all | solution.py:64
  283.2 11.6 %all-to-all-start.6 = ((f32[1,512,128]{2,0,1:T(1,128)}), f32[1,512,128]{2,0,1:T(1,128)S(1)}, u32[]{:S(2)}, u32[]{:S(2)}) async-start(f32[1,512,128]{2,0,1:T(1,128)} %bitcast.82), calls=%async_computation.6 | async-start | bytes 524288 | tf_op jit(solution)/shard_map/all_to_all | solution.py:65
  294.8 35.8 %all-to-all-start.3 = ((f32[1,512,128]{2,0,1:T(1,128)}), f32[1,512,128]{2,0,1:T(1,128)S(1)}, u32[]{:S(2)}, u32[]{:S(2)}) async-start(f32[1,512,128]{2,0,1:T(1,128)} %bitcast.44), calls=%async_computation.3 | async-start | bytes 524288 | tf_op jit(solution)/shard_map/all_to_all | solution.py:65
  330.6 42.0 %all-to-all-start = ((f32[1,512,128]{2,0,1:T(1,128)}), f32[1,512,128]{2,0,1:T(1,128)S(1)}, u32[]{:S(2)}, u32[]{:S(2)}) async-start(f32[1,512,128]{2,0,1:T(1,128)} %bitcast.6), calls=%async_computation | async-start | bytes 524288 | tf_op jit(solution)/shard_map/all_to_all | solution.py:65
